TPU v7x, 32 devices: a whole 2x2x4 slice. The times are simulated.
32 devices in a mesh: dp: 8 (over z, x), ctx: 4 (over y, core).
Axes of the slice: x: 2, y: 2, z: 4, core: 2. Of those that a mesh axis runs over, the one named last changes fastest.
Arguments:
- inputs: bfloat16 [8, 2048, 768], P('dp', 'ctx'), may hold values from -6 to 6
- segments: int32 [8, 2048], P('dp'), may hold values from 0 to 34, as said below
- qkv_weight: bfloat16 [768, 2304], P(('dp', 'ctx')), may hold values from -0.21875 to 0.21875
- query_value_bias: bfloat16 [1536], P(('dp', 'ctx')), may hold values from -3 to 3
- output_weight: bfloat16 [768, 768], P(('dp', 'ctx')), may hold values from -1.75 to 1.75
- output_bias: bfloat16 [768], P(('dp', 'ctx')), may hold values from -3 to 3
- attention_gain: bfloat16 [768], P(('dp', 'ctx')), may hold values from 0.25 to 1.75
- attention_shift: bfloat16 [768], P(('dp', 'ctx')), may hold values from -2 to 2
- up_weight: bfloat16 [768, 3072], P(('dp', 'ctx')), may hold values from -0.21875 to 0.21875
- up_bias: bfloat16 [3072], P(('dp', 'ctx')), may hold values from -3 to 3
- down_weight: bfloat16 [3072, 768], P(('dp', 'ctx')), may hold values from -0.109375 to 0.109375
- down_bias: bfloat16 [768], P(('dp', 'ctx')), may hold values from -3 to 3
- final_gain: bfloat16 [768], P(('dp', 'ctx')), may hold values from 0.25 to 1.75
- final_shift: bfloat16 [768], P(('dp', 'ctx')), may hold values from -2 to 2
- cotangent: bfloat16 [8, 2048, 768], P('dp', 'ctx'), may hold values from -6 to 6
Outputs:
- output: bfloat16 [8, 2048, 768], P('dp', 'ctx')
- input_grad: float32 [8, 2048, 768], P('dp', 'ctx')
- qkv_weight_grad: float32 [768, 2304], P(('dp', 'ctx'))
- query_value_bias_grad: float32 [1536], P(('dp', 'ctx'))
- output_weight_grad: float32 [768, 768], P(('dp', 'ctx'))
- output_bias_grad: float32 [768], P(('dp', 'ctx'))
- attention_gain_grad: float32 [768], P(('dp', 'ctx'))
- attention_shift_grad: float32 [768], P(('dp', 'ctx'))
- up_weight_grad: float32 [768, 3072], P(('dp', 'ctx'))
- up_bias_grad: float32 [3072], P(('dp', 'ctx'))
- down_weight_grad: float32 [3072, 768], P(('dp', 'ctx'))
- down_bias_grad: float32 [768], P(('dp', 'ctx'))
- final_gain_grad: float32 [768], P(('dp', 'ctx'))
- final_shift_grad: float32 [768], P(('dp', 'ctx'))
Inputs may be any that keep to these rules, and one draw needn't show every extreme that they name: `segments`: in each sequence, segment numbers count its whole documents from 1 in order of position; each document spans 60 to 800 positions; the positions after the last whole document, one or more, are 0. The first sequence is packed with documents of exactly 60 positions.
All inputs are finite; a program needn't handle non-finite values.
Results may differ from a plain program's by a relative error of at most 0.017.
Values may be sent and summed in bfloat16 or wider, within the bound.
No kernel may reach another device: no remote copies, remote signals or barrier semaphores. Data moves between devices by JAX's collectives and lax.ppermute only.
A program may use at most 128 MiB of HBM per device.

v0:
```python
import jax
import jax.numpy as jnp
from jax import lax
from jax.sharding import PartitionSpec as P

HEADS = 12
HEAD_DIM = 64
MASKED = -1000000000.0


def layer_norm(rows, gain, shift):
    center = jnp.mean(rows, axis=-1, keepdims=True)
    centred = rows - center
    spread = jnp.mean(centred * centred, axis=-1, keepdims=True)
    return centred * lax.rsqrt(spread + 1e-06) * gain + shift


def exact_gelu(values):
    return jax.nn.gelu(values, approximate=False)


def inner_rows(left, right):
    return lax.dot_general(
        left, right, (((0,), (0,)), ((), ())), preferred_element_type=jnp.float32
    )


def times_transpose(left, right):
    return lax.dot_general(
        left, right, (((1,), (1,)), ((), ())), preferred_element_type=jnp.float32
    )


def shards(
    inputs,
    segments,
    qkv_weight,
    query_value_bias,
    output_weight,
    output_bias,
    attention_gain,
    attention_shift,
    up_weight,
    up_bias,
    down_weight,
    down_bias,
    final_gain,
    final_shift,
    cotangent,
):
    gathered = (
        lax.all_gather(qkv_weight, ("dp", "ctx"), axis=0, tiled=True),
        lax.all_gather(query_value_bias, ("dp", "ctx"), axis=0, tiled=True),
        lax.all_gather(output_weight, ("dp", "ctx"), axis=0, tiled=True),
        lax.all_gather(output_bias, ("dp", "ctx"), axis=0, tiled=True),
        lax.all_gather(attention_gain, ("dp", "ctx"), axis=0, tiled=True),
        lax.all_gather(attention_shift, ("dp", "ctx"), axis=0, tiled=True),
        lax.all_gather(up_weight, ("dp", "ctx"), axis=0, tiled=True),
        lax.all_gather(up_bias, ("dp", "ctx"), axis=0, tiled=True),
        lax.all_gather(down_weight, ("dp", "ctx"), axis=0, tiled=True),
        lax.all_gather(down_bias, ("dp", "ctx"), axis=0, tiled=True),
        lax.all_gather(final_gain, ("dp", "ctx"), axis=0, tiled=True),
        lax.all_gather(final_shift, ("dp", "ctx"), axis=0, tiled=True),
    )
    (
        qkv_full,
        bias_qv,
        out_full,
        bias_out,
        gain_one,
        shift_one,
        up_full,
        bias_up,
        down_full,
        bias_down,
        gain_two,
        shift_two,
    ) = gathered
    seq_count, group, width = inputs.shape
    row_total = seq_count * group
    seq_len = group * lax.axis_size("ctx")
    flat_in = inputs.reshape(row_total, width)
    zero_keys = jnp.zeros((width,), jnp.float32)
    bias_f32 = bias_qv.astype(jnp.float32)
    qkv_bias = jnp.concatenate([bias_f32[:width], zero_keys, bias_f32[width:]])
    qkv_rows = jnp.dot(flat_in, qkv_full, preferred_element_type=jnp.float32) + qkv_bias
    queries = (
        (qkv_rows[:, :width] * 0.125)
        .astype(jnp.bfloat16)
        .reshape(seq_count, group, HEADS, HEAD_DIM)
    )
    key_rows = qkv_rows[:, width : 2 * width].astype(jnp.bfloat16).reshape(seq_count, group, width)
    value_rows = qkv_rows[:, 2 * width :].astype(jnp.bfloat16).reshape(seq_count, group, width)
    offset = lax.axis_index("ctx") * group
    query_seg = lax.dynamic_slice_in_dim(segments, offset, group, 1)

    def allowed_mask(key_seg):
        return (query_seg[:, :, None, None] == key_seg[:, None, None, :]) & (
            key_seg[:, None, None, :] > 0
        )

    def block_pieces(piece_keys, piece_values, begin, block_size):
        block_keys = lax.dynamic_slice_in_dim(piece_keys, begin, block_size, 1).reshape(
            seq_count, block_size, HEADS, HEAD_DIM
        )
        block_values = lax.dynamic_slice_in_dim(piece_values, begin, block_size, 1).reshape(
            seq_count, block_size, HEADS, HEAD_DIM
        )
        key_seg = lax.dynamic_slice_in_dim(segments, begin, block_size, 1)
        scores = jnp.einsum(
            "bqhd,bkhd->bqhk", queries, block_keys, preferred_element_type=jnp.float32
        )
        masked = jnp.where(allowed_mask(key_seg), scores, MASKED)
        return (block_keys, block_values, masked)

    start_state = (
        jnp.zeros((seq_count, group, HEADS, HEAD_DIM), jnp.float32),
        jnp.zeros((seq_count, group, HEADS), jnp.float32),
        jnp.zeros((seq_count, group, HEADS), jnp.float32),
    )
    piece_keys = lax.all_gather(key_rows, "ctx", axis=1, tiled=True)
    piece_values = lax.all_gather(value_rows, "ctx", axis=1, tiled=True)
    span = piece_keys.shape[1]
    block_size = 512

    def forward_one_block(state, block_index):
        running, row_max, row_sum = state
        begin = block_index * block_size
        block_keys, block_values, masked = block_pieces(piece_keys, piece_values, begin, block_size)
        new_max = jnp.maximum(row_max, jnp.max(masked, axis=-1))
        rescale = jnp.exp(row_max - new_max)
        weights = jnp.exp(masked - new_max[..., None])
        row_sum = row_sum * rescale + jnp.sum(weights, axis=-1)
        running = running * rescale[..., None] + jnp.einsum(
            "bqhk,bkhd->bqhd",
            weights.astype(jnp.bfloat16),
            block_values,
            preferred_element_type=jnp.float32,
        )
        return ((running, new_max, row_sum), None)

    state, unused = lax.scan(
        forward_one_block, start_state, jnp.arange(span // block_size, dtype=jnp.int32)
    )
    running, row_max, row_sum = state
    safe_sum = jnp.where(query_seg[:, :, None] > 0, row_sum, 1.0)
    attended = running / safe_sum[..., None]
    mixed_low = attended.reshape(row_total, width).astype(jnp.bfloat16)
    resid_one = (
        flat_in.astype(jnp.float32)
        + jnp.dot(mixed_low, out_full, preferred_element_type=jnp.float32)
        + bias_out.astype(jnp.float32)
    )
    normed, first_back = jax.vjp(
        layer_norm, resid_one, gain_one.astype(jnp.float32), shift_one.astype(jnp.float32)
    )
    normed_low = normed.astype(jnp.bfloat16)
    hidden_pre = jnp.dot(normed_low, up_full, preferred_element_type=jnp.float32) + bias_up.astype(
        jnp.float32
    )
    hidden_low = exact_gelu(hidden_pre).astype(jnp.bfloat16)
    resid_two = (
        normed
        + jnp.dot(hidden_low, down_full, preferred_element_type=jnp.float32)
        + bias_down.astype(jnp.float32)
    )
    result, final_back = jax.vjp(
        layer_norm, resid_two, gain_two.astype(jnp.float32), shift_two.astype(jnp.float32)
    )
    output = result.astype(jnp.bfloat16).reshape(seq_count, group, width)
    regathered = (
        lax.all_gather(qkv_weight, ("dp", "ctx"), axis=0, tiled=True),
        lax.all_gather(query_value_bias, ("dp", "ctx"), axis=0, tiled=True),
        lax.all_gather(output_weight, ("dp", "ctx"), axis=0, tiled=True),
        lax.all_gather(output_bias, ("dp", "ctx"), axis=0, tiled=True),
        lax.all_gather(attention_gain, ("dp", "ctx"), axis=0, tiled=True),
        lax.all_gather(attention_shift, ("dp", "ctx"), axis=0, tiled=True),
        lax.all_gather(up_weight, ("dp", "ctx"), axis=0, tiled=True),
        lax.all_gather(up_bias, ("dp", "ctx"), axis=0, tiled=True),
        lax.all_gather(down_weight, ("dp", "ctx"), axis=0, tiled=True),
        lax.all_gather(down_bias, ("dp", "ctx"), axis=0, tiled=True),
        lax.all_gather(final_gain, ("dp", "ctx"), axis=0, tiled=True),
        lax.all_gather(final_shift, ("dp", "ctx"), axis=0, tiled=True),
    )
    qkv_back = regathered[0]
    out_back = regathered[2]
    up_back = regathered[6]
    down_back = regathered[8]
    grad_out = cotangent.reshape(row_total, width).astype(jnp.float32)
    grad_resid_two, final_gain_grad, final_shift_grad = final_back(grad_out)
    grad_down_in = grad_resid_two.astype(jnp.bfloat16)
    down_bias_grad = jnp.sum(grad_down_in.astype(jnp.float32), axis=0)
    down_weight_grad = inner_rows(hidden_low, grad_down_in)
    grad_hidden = times_transpose(grad_down_in, down_back)
    unused_value, gelu_pull = jax.vjp(exact_gelu, hidden_pre)
    grad_pre = gelu_pull(grad_hidden)[0].astype(jnp.bfloat16)
    up_bias_grad = jnp.sum(grad_pre.astype(jnp.float32), axis=0)
    up_weight_grad = inner_rows(normed_low, grad_pre)
    grad_normed = grad_resid_two + times_transpose(grad_pre, up_back)
    grad_resid_one, attention_gain_grad, attention_shift_grad = first_back(grad_normed)
    grad_mix_in = grad_resid_one.astype(jnp.bfloat16)
    output_bias_grad = jnp.sum(grad_mix_in.astype(jnp.float32), axis=0)
    output_weight_grad = inner_rows(mixed_low, grad_mix_in)
    grad_mixed = (
        times_transpose(grad_mix_in, out_back)
        .astype(jnp.bfloat16)
        .reshape(seq_count, group, HEADS, HEAD_DIM)
    )
    delta_rows = jnp.sum(grad_mixed.astype(jnp.float32) * attended, axis=-1)
    back_state = (
        jnp.zeros((seq_count, group, HEADS, HEAD_DIM), jnp.float32),
        jnp.zeros((seq_count, seq_len, width), jnp.float32),
        jnp.zeros((seq_count, seq_len, width), jnp.float32),
    )
    backward_piece_keys = lax.all_gather(key_rows, "ctx", axis=1, tiled=True)
    backward_piece_values = lax.all_gather(value_rows, "ctx", axis=1, tiled=True)
    span = backward_piece_keys.shape[1]
    backward_block_size = 512

    def backward_one_block(state, block_index):
        grad_query, grad_keys, grad_values = state
        begin = block_index * backward_block_size
        block_keys, block_values, masked = block_pieces(
            backward_piece_keys, backward_piece_values, begin, backward_block_size
        )
        probs = jnp.exp(masked - row_max[..., None]) / safe_sum[..., None]
        grad_probs = jnp.einsum(
            "bqhd,bkhd->bqhk", grad_mixed, block_values, preferred_element_type=jnp.float32
        )
        grad_scores = (probs * (grad_probs - delta_rows[..., None])).astype(jnp.bfloat16)
        grad_query = grad_query + jnp.einsum(
            "bqhk,bkhd->bqhd", grad_scores, block_keys, preferred_element_type=jnp.float32
        )
        key_part = jnp.einsum(
            "bqhk,bqhd->bkhd", grad_scores, queries, preferred_element_type=jnp.float32
        ).reshape(seq_count, backward_block_size, width)
        value_part = jnp.einsum(
            "bqhk,bqhd->bkhd",
            probs.astype(jnp.bfloat16),
            grad_mixed,
            preferred_element_type=jnp.float32,
        ).reshape(seq_count, backward_block_size, width)
        grad_keys = lax.dynamic_update_slice_in_dim(grad_keys, key_part, begin, 1)
        grad_values = lax.dynamic_update_slice_in_dim(grad_values, value_part, begin, 1)
        return ((grad_query, grad_keys, grad_values), None)

    state, unused = lax.scan(
        backward_one_block, back_state, jnp.arange(span // backward_block_size, dtype=jnp.int32)
    )
    grad_query, grad_keys, grad_values = state
    own_keys, own_values = (
        lax.psum_scatter(
            grad_keys.astype(jnp.bfloat16), "ctx", scatter_dimension=1, tiled=True
        ).astype(jnp.float32),
        lax.psum_scatter(
            grad_values.astype(jnp.bfloat16), "ctx", scatter_dimension=1, tiled=True
        ).astype(jnp.float32),
    )
    grad_qkv = jnp.concatenate(
        [
            grad_query.reshape(row_total, width) * 0.125,
            own_keys.reshape(row_total, width),
            own_values.reshape(row_total, width),
        ],
        axis=1,
    ).astype(jnp.bfloat16)
    column_sums = jnp.sum(grad_qkv.astype(jnp.float32), axis=0)
    qv_bias_grad = jnp.concatenate([column_sums[:width], column_sums[2 * width :]])
    qkv_weight_grad = inner_rows(flat_in, grad_qkv)
    input_grad = (grad_resid_one + times_transpose(grad_qkv, qkv_back)).reshape(
        seq_count, group, width
    )
    shares = (
        lax.psum_scatter(qkv_weight_grad, ("dp", "ctx"), scatter_dimension=0, tiled=True),
        lax.psum_scatter(qv_bias_grad, ("dp", "ctx"), scatter_dimension=0, tiled=True),
        lax.psum_scatter(output_weight_grad, ("dp", "ctx"), scatter_dimension=0, tiled=True),
        lax.psum_scatter(output_bias_grad, ("dp", "ctx"), scatter_dimension=0, tiled=True),
        lax.psum_scatter(attention_gain_grad, ("dp", "ctx"), scatter_dimension=0, tiled=True),
        lax.psum_scatter(attention_shift_grad, ("dp", "ctx"), scatter_dimension=0, tiled=True),
        lax.psum_scatter(up_weight_grad, ("dp", "ctx"), scatter_dimension=0, tiled=True),
        lax.psum_scatter(up_bias_grad, ("dp", "ctx"), scatter_dimension=0, tiled=True),
        lax.psum_scatter(down_weight_grad, ("dp", "ctx"), scatter_dimension=0, tiled=True),
        lax.psum_scatter(down_bias_grad, ("dp", "ctx"), scatter_dimension=0, tiled=True),
        lax.psum_scatter(final_gain_grad, ("dp", "ctx"), scatter_dimension=0, tiled=True),
        lax.psum_scatter(final_shift_grad, ("dp", "ctx"), scatter_dimension=0, tiled=True),
    )
    return (
        output,
        input_grad,
        shares[0],
        shares[1],
        shares[2],
        shares[3],
        shares[4],
        shares[5],
        shares[6],
        shares[7],
        shares[8],
        shares[9],
        shares[10],
        shares[11],
    )


def solution(mesh):
    placed = (
        P("dp", "ctx", None),
        P("dp", None),
        P(("dp", "ctx"), None),
        P(("dp", "ctx")),
        P(("dp", "ctx"), None),
        P(("dp", "ctx")),
        P(("dp", "ctx")),
        P(("dp", "ctx")),
        P(("dp", "ctx"), None),
        P(("dp", "ctx")),
        P(("dp", "ctx"), None),
        P(("dp", "ctx")),
        P(("dp", "ctx")),
        P(("dp", "ctx")),
        P("dp", "ctx", None),
    )
    return jax.shard_map(
        shards,
        mesh=mesh,
        in_specs=placed,
        out_specs=(
            P("dp", "ctx", None),
            P("dp", "ctx", None),
            P(("dp", "ctx"), None),
            P(("dp", "ctx")),
            P(("dp", "ctx"), None),
            P(("dp", "ctx")),
            P(("dp", "ctx")),
            P(("dp", "ctx")),
            P(("dp", "ctx"), None),
            P(("dp", "ctx")),
            P(("dp", "ctx"), None),
            P(("dp", "ctx")),
            P(("dp", "ctx")),
            P(("dp", "ctx")),
        ),
        check_vma=False,
    )
```

profile of v0, /device:TPU:0, one launch (start us, length us, event | category | flops | bytes accessed | tf_op | source)
XLA Modules:
  0.0 1081.2 jit_solution(16484203945727431277)
XLA Ops:
  14.7 42.5 %all-reduce.17 = (bf16[1536]{0:T(1024)(128)(2,1)S(1)}, bf16[768]{0:T(1024)(128)(2,1)S(1)}, bf16[768]{0:T(1024)(128)(2,1)S(1)}, bf16[768]{0:T(1024)(128)(2,1)S(1)...) all-reduce(bf16[1536]{0:T(1024)(128)(2,1)S(1)} %dynamic-update-slic, ...), channel_id=1, replica_groups=mesh['dp'=8,'ctx'=4] {'dp','ctx'}, use_global_device_ids=true, to_apply=%add | all-reduce | flops 9216 | bytes 36864
  57.2 16.5 %all-gather.9.cloned.1.call-done = bf16[768,2304]{1,0:T(8,128)(2,1)} async-done(((bf16[24,2304]{1,0:T(8,128)(2,1)}), bf16[768,2304]{1,0:T(8,128)(2,1)}) %all-gather.9.cloned.1.call-update) | async-done | bytes 3538960 | tf_op jit(solution)/shard_map/all_gather | solution.py:52
  86.7 22.2 %all-gather.17.cloned.1.call-done = bf16[2048,768]{1,0:T(8,128)(2,1)} async-done(((bf16[512,768]{1,0:T(8,128)(2,1)}), bf16[2048,768]{1,0:T(8,128)(2,1)}) %all-gather.17.cloned.1.call-update) | async-done | bytes 3145744 | tf_op jit(solution)/shard_map/all_gather | solution.py:121
  113.6 26.0 %all-gather.19.cloned.1.call-done = bf16[2048,768]{1,0:T(8,128)(2,1)} async-done(((bf16[512,768]{1,0:T(8,128)(2,1)}), bf16[2048,768]{1,0:T(8,128)(2,1)}) %all-gather.19.cloned.1.call-update) | async-done | bytes 3145744 | tf_op jit(solution)/shard_map/all_gather | solution.py:122
  144.3 83.3 %while.30 = (s32[]{:T(128)}, f32[1,512,12,64]{1,3,2,0:T(8,128)S(1)}, f32[1,512,12]{1,2,0:T(8,128)S(1)}, f32[1,512,12]{1,2,0:T(8,128)S(1)}, s32[1,512]{1,0:T(1,12...) while((s32[]{:T(128)}, ...), condition=%wide.region_3.4_spmd.clone, body=%wide.region_0.3_spmd.clone.sunk | while | flops 832213504 | bytes 98184608 | solution.py:142
  153.8 6.9 fusion.118
  174.6 6.9 fusion.118
  195.4 6.9 fusion.118
  216.2 6.9 fusion.118
  232.7 28.9 %all-gather.13.cloned.1.call-done = bf16[768,3072]{1,0:T(8,128)(2,1)} async-done(((bf16[24,3072]{1,0:T(8,128)(2,1)}), bf16[768,3072]{1,0:T(8,128)(2,1)}) %all-gather.13.cloned.1.call-update) | async-done | bytes 4718608 | tf_op jit(solution)/shard_map/all_gather | solution.py:58
  261.6 21.0 %multiply_convert_fusion = (bf16[512,3072]{1,0:T(8,128)(2,1)}, f32[512,3072]{1,0:T(8,128)}, f32[512,3072]{1,0:T(8,128)}) fusion(f32[3072]{0:T(1024)S(1)} %convert_element_type.115, bf16[768,3072]{1,0:T(8,128)(2,1)} %all-gather.13.cloned.1.call-done, f32[512,768]{1,0:T(8,128)} %copy-done.11, f32[768]{0:T(1024)S(1)} %convert_element_type.113, ...), kind=kOutput, calls=%fused_computation.55 | convolution fusion | flops 2521694208 | bytes 22042624 | tf_op jit(solution)/shard_map/dot_general | solution.py:158
  282.6 43.6 %all-gather.15.cloned.1.call-done = bf16[3072,768]{1,0:T(8,128)(2,1)} async-done(((bf16[96,768]{1,0:T(8,128)(2,1)}), bf16[3072,768]{1,0:T(8,128)(2,1)}) %all-gather.15.cloned.1.call-update) | async-done | bytes 4718608 | tf_op jit(solution)/shard_map/all_gather | solution.py:60
  337.0 9.2 convert_reduce_fusion
  362.3 121.7 %while.31 = (s32[]{:T(128)}, f32[1,512,12,64]{1,3,2,0:T(8,128)}, bf16[1,2048,768]{1,2,0:T(8,128)(2,1)}, bf16[1,2048,768]{1,2,0:T(8,128)(2,1)}, s32[4]{0:T(128)S(...) while((s32[]{:T(128)}, f32[1,512,12,64]{1,3,2,0:T(8,128)}, ...), condition=%wide.region_14.15_spmd.clone, body=%wide.region_13.14_spmd.clone.sunk | while | flops 2046034432 | bytes 124390832 | solution.py:247
  487.8 7.3 fusion.52
  496.2 8.2 fusion.66
  506.0 14.3 %reduce-scatter.9.cloned.1.call-done = bf16[1,512,768]{1,2,0:T(8,128)(2,1)} async-done(((bf16[1,2048,768]{1,2,0:T(8,128)(2,1)}), bf16[1,512,768]{1,2,0:T(8,128)(2,1)}) %reduce-scatter.9.cloned.1.call-update) | async-done | bytes 786448 | tf_op jit(solution)/shard_map/reduce_scatter | solution.py:252
  520.3 40.3 %reduce-scatter.11.cloned.1.call-done = bf16[1,512,768]{1,2,0:T(8,128)(2,1)} async-done(((bf16[1,2048,768]{1,2,0:T(8,128)(2,1)}), bf16[1,512,768]{1,2,0:T(8,128)(2,1)}) %reduce-scatter.11.cloned.1.call-update) | async-done | bytes 786448 | tf_op jit(solution)/shard_map/reduce_scatter | solution.py:255
  566.8 8.0 copy.68
  577.9 40.2 %all-reduce.16 = (f32[1536]{0:T(1024)S(1)}, f32[768]{0:T(1024)S(1)}, f32[768]{0:T(1024)S(1)}, f32[768]{0:T(1024)S(1)}, f32[3072]{0:T(1024)S(1)}, /*index=5*/f32[...) all-reduce(f32[1536]{0:T(1024)S(1)} %pad_maximum_fusion.2, ...), channel_id=7, replica_groups=mesh['dp'=8,'ctx'=4] {'dp','ctx'}, use_global_device_ids=true, to_apply=%region_19.20.clone | all-reduce | flops 9216 | bytes 73728
  628.6 37.6 %reduce-scatter.13.cloned.1.call-done = f32[24,768]{1,0:T(8,128)} async-done(((f32[768,768]{1,0:T(8,128)}), f32[24,768]{1,0:T(8,128)}) %reduce-scatter.13.cloned.1.call-update) | async-done | bytes 73744 | tf_op jit(solution)/shard_map/reduce_scatter | solution.py:276
  666.2 141.6 %reduce-scatter.15.cloned.1.call-done = f32[24,3072]{1,0:T(8,128)} async-done(((f32[768,3072]{1,0:T(8,128)}), f32[24,3072]{1,0:T(8,128)}) %reduce-scatter.15.cloned.1.call-update) | async-done | bytes 294928 | tf_op jit(solution)/shard_map/reduce_scatter | solution.py:280
  807.8 141.7 %reduce-scatter.17.cloned.1.call-done = f32[96,768]{1,0:T(8,128)} async-done(((f32[3072,768]{1,0:T(8,128)}), f32[96,768]{1,0:T(8,128)}) %reduce-scatter.17.cloned.1.call-update) | async-done | bytes 294928 | tf_op jit(solution)/shard_map/reduce_scatter | solution.py:282
  949.5 124.7 %reduce-scatter.19.cloned.1.call-done = f32[24,2304]{1,0:T(8,128)} async-done(((f32[768,2304]{1,0:T(8,128)}), f32[24,2304]{1,0:T(8,128)}) %reduce-scatter.19.cloned.1.call-update) | async-done | bytes 221200
  (351 shorter events, 258.9 us)
Async XLA Ops:
  7.2 66.6 %all-gather.9.cloned.1.call-start = ((), (), s32[]{:S(2)}) async-start(), calls=%async_computation.6 | async-start | bytes 3649536 | tf_op jit(solution)/shard_map/all_gather | solution.py:52
  7.9 100.9 %all-gather.17.cloned.1.call-start = ((), (), s32[]{:S(2)}) async-start(), calls=%async_computation.15 | async-start | bytes 3932160 | tf_op jit(solution)/shard_map/all_gather | solution.py:121
  81.4 58.1 %all-gather.19.cloned.1.call-start = ((), (), s32[]{:S(2)}) async-start(), calls=%async_computation.16 | async-start | bytes 3932160 | tf_op jit(solution)/shard_map/all_gather | solution.py:122
  82.1 145.7 %all-gather.11.cloned.1.call-start = ((), (), s32[]{:S(2)}) async-start(), calls=%async_computation.7 | async-start | bytes 1216512 | tf_op jit(solution)/shard_map/all_gather | solution.py:54
  82.7 178.9 %all-gather.13.cloned.1.call-start = ((), (), s32[]{:S(2)}) async-start(), calls=%async_computation.8 | async-start | bytes 4866048 | tf_op jit(solution)/shard_map/all_gather | solution.py:58
  83.3 242.9 %all-gather.15.cloned.1.call-start = ((), (), s32[]{:S(2)}) async-start(), calls=%async_computation.9 | async-start | bytes 4866048 | tf_op jit(solution)/shard_map/all_gather | solution.py:60
  83.9 436.4 %reduce-scatter.9.cloned.1.call-start = ((), (), s32[]{:S(2)}) async-start(), calls=%async_computation.10 | async-start | bytes 3932160 | tf_op jit(solution)/shard_map/reduce_scatter | solution.py:252
  84.7 265.2 %copy-start.29 = (f32[768]{0:T(1024)}, f32[768]{0:T(1024)S(1)}, u32[]{:S(2)}) copy-start(f32[768]{0:T(1024)S(1)} %convert_element_type.112) | copy-start | bytes 9220
  84.8 241.5 %copy-start.36 = (f32[768]{0:T(1024)}, f32[768]{0:T(1024)S(1)}, u32[]{:S(2)}) copy-start(f32[768]{0:T(1024)S(1)} %convert_element_type.113) | copy-start | bytes 9220
  216.2 8.3 copy-start
  230.6 119.3 %copy-start.24 = (f32[512]{0:T(512)}, f32[512]{0:T(512)S(1)}, u32[]{:S(2)}) copy-start(f32[512]{0:T(512)S(1)} %broadcast_multiply_fusion.1) | copy-start | bytes 6148
  232.0 117.9 %copy-start.32 = (f32[512]{0:T(512)}, f32[512]{0:T(512)S(1)}, u32[]{:S(2)}) copy-start(f32[512]{0:T(512)S(1)} %fusion.50) | copy-start | bytes 6148
  336.0 10.2 slice-start
  336.8 9.4 copy-start.20
  337.0 9.2 copy-start.12
  337.0 9.2 slice-start.1
  484.1 76.5 %reduce-scatter.11.cloned.1.call-start = ((), (), s32[]{:S(2)}) async-start(), calls=%async_computation.11 | async-start | bytes 3932160 | tf_op jit(solution)/shard_map/reduce_scatter | solution.py:255
  484.9 181.3 %reduce-scatter.13.cloned.1.call-start = ((), (), s32[]{:S(2)}) async-start(), calls=%async_computation.12 | async-start | bytes 2433024 | tf_op jit(solution)/shard_map/reduce_scatter | solution.py:276
  487.7 320.2 %reduce-scatter.15.cloned.1.call-start = ((), (), s32[]{:S(2)}) async-start(), calls=%async_computation.13 | async-start | bytes 9732096 | tf_op jit(solution)/shard_map/reduce_scatter | solution.py:280
  495.1 454.4 %reduce-scatter.17.cloned.1.call-start = ((), (), s32[]{:S(2)}) async-start(), calls=%async_computation.14 | async-start | bytes 9732096 | tf_op jit(solution)/shard_map/reduce_scatter | solution.py:282
  504.4 56.2 %copy-start.42 = (bf16[1,512,768]{2,1,0:T(8,128)(2,1)S(1)}, bf16[1,512,768]{2,1,0:T(8,128)(2,1)}, u32[]{:S(2)}) copy-start(bf16[1,512,768]{2,1,0:T(8,128)(2,1)} %param.19) | copy-start | bytes 2359300
  504.4 569.8 %reduce-scatter.19.cloned.1.call-start = ((), (), s32[]{:S(2)}) async-start(), calls=%async_computation.17 | async-start | bytes 7299072
  574.9 48.0 %copy-start.15 = (f32[512,768]{1,0:T(8,128)S(1)}, f32[512,768]{1,0:T(8,128)}, u32[]{:S(2)}) copy-start(f32[512,768]{1,0:T(8,128)} %copy-done.14) | copy-start | bytes 4718596
  574.9 47.9 %copy-start.35 = (f32[512]{0:T(512)S(1)}, f32[512]{0:T(512)}, u32[]{:S(2)}) copy-start(f32[512]{0:T(512)} %copy-done.34) | copy-start | bytes 6148
  (66 other events, 215.2 us)
Sparse Core Ops, SparseCore 0:
  10.9 62.7 all-gather.8
  81.5 27.2 all-gather.16
  111.0 28.4 all-gather.18
  142.3 53.9 all-gather.10
  199.1 62.4 all-gather.12
  264.3 61.8 all-gather.14
  484.2 36.0 reduce-scatter.8
  522.8 37.7 reduce-scatter.10
  566.4 99.7 reduce-scatter.12
  672.5 135.2 reduce-scatter.14
  814.3 135.1 reduce-scatter.16
  955.6 118.5 reduce-scatter.18
where the time goes:
time: 1090 us; the launch traced here: 1080 us
  waiting for transfers between devices  641 us (59%)
  matrix products  208 us (19%)
  local copies, waits for them, and re-layouts  85 us (8%)
  blocking collectives  82.7 us (8%)
  other arithmetic  42.1 us (4%)
  between operations  15 us (1%)
    reduce_scatter x1, waiting for transfers between devices, shards(): lax.psum_scatter(down_weight_grad, ('dp', 'ctx'), scatter_dimension=0, ti...  142 us
    reduce_scatter x1, waiting for transfers between devices, shards(): lax.psum_scatter(up_weight_grad, ('dp', 'ctx'), scatter_dimension=0, tile...  142 us
    unnamed x13, waiting for transfers between devices  128 us
    unnamed x2, blocking collectives  82.7 us
    all_gather x1, waiting for transfers between devices, shards(): lax.all_gather(down_weight, ('dp', 'ctx'), axis=0, tiled=True)  43.6 us
    reduce_scatter x1, waiting for transfers between devices, shards(): lax.psum_scatter(grad_values.astype(jnp.bfloat16), 'ctx', scatter_dimensi...  40.3 us
    dot_general x8, matrix products, block_pieces(): jnp.einsum('bqhd,bkhd->bqhk', queries, block_keys, preferred_element_type...  38.8 us
    reduce_scatter x1, waiting for transfers between devices, shards(): lax.psum_scatter(output_weight_grad, ('dp', 'ctx'), scatter_dimension=0,...  37.6 us
  transfers between devices with their start and end apart: 12, of which 11 were waited for; matrix products, arithmetic and copies ran while one was open for 15% of the time, Pallas kernels for 0%

commit v1 on v0

--- a/solution.py
+++ b/solution.py
@@ -118,8 +118,12 @@
         jnp.zeros((seq_count, group, HEADS), jnp.float32),
         jnp.zeros((seq_count, group, HEADS), jnp.float32),
     )
-    piece_keys = lax.all_gather(key_rows, "ctx", axis=1, tiled=True)
-    piece_values = lax.all_gather(value_rows, "ctx", axis=1, tiled=True)
+    recast_frames = lambda block_in, original, axis_id: jnp.split(
+        lax.all_gather(jnp.concatenate([block_in, original], axis=0), axis_id, axis=1, tiled=True),
+        [block_in.shape[0]],
+        axis=0,
+    )
+    piece_keys, piece_values = recast_frames(key_rows, original=value_rows, axis_id="ctx")
     span = piece_keys.shape[1]
     block_size = 512
 

time: 1090 us -> 1120 us (1.028)
  matrix products: 208 us -> 251 us
    dot_general x4, matrix products: 12.4 us -> 36.4 us  [forward_one_block(): jnp.einsum('bqhk,bkhd->bqhd', weights.astype(jnp.bfloat16), block_values,...]
    all_gather x1, waiting for transfers between devices: 28.9 us -> 7.64 us  [shards(): lax.all_gather(up_weight, ('dp', 'ctx'), axis=0, tiled=True)]
    all_gather x2 -> x3, waiting for transfers between devices: 48.2 us -> 67.7 us  [the longest x1 40.5 us: shards(): lax.all_gather(jnp.concatenate([block_in, original], axis=0), axis_id, ax...]
    dot_general x8, matrix products: 38.8 us -> 51.4 us  [block_pieces(): jnp.einsum('bqhd,bkhd->bqhk', queries, block_keys, preferred_element_type...]
    dot_general x4, matrix products: 19.9 us -> 31.2 us  [backward_one_block(): jnp.einsum('bqhk,bqhd->bkhd', probs.astype(jnp.bfloat16), grad_mixed, pre...]
    unnamed x103 -> x99, local copies, waits for them, and re-layouts: 35.2 us -> 24.9 us
    unnamed x13 -> x14, waiting for transfers between devices: 128 us -> 129 us
  transfers between devices with their start and end apart: 12 -> 13, of which waited for: 11 -> 11; matrix products, arithmetic and copies ran while one was open for 15% -> 19% of each run, Pallas kernels for 0% -> 0%
where the time goes in v1:
time: 1120 us
  waiting for transfers between devices  642 us (57%)
  matrix products  251 us (22%)
  blocking collectives  82.7 us (7%)
  local copies, waits for them, and re-layouts  78.2 us (7%)
  other arithmetic  43.1 us (4%)
  between operations  14.8 us (1%)
    reduce_scatter x1, waiting for transfers between devices, shards(): lax.psum_scatter(up_weight_grad, ('dp', 'ctx'), scatter_dimension=0, tile...  142 us
    reduce_scatter x1, waiting for transfers between devices, shards(): lax.psum_scatter(down_weight_grad, ('dp', 'ctx'), scatter_dimension=0, ti...  141 us
    unnamed x14, waiting for transfers between devices  129 us
    unnamed x2, blocking collectives  82.7 us
    dot_general x8, matrix products, block_pieces(): jnp.einsum('bqhd,bkhd->bqhk', queries, block_keys, preferred_element_type...  51.4 us
    all_gather x1, waiting for transfers between devices, shards(): lax.all_gather(down_weight, ('dp', 'ctx'), axis=0, tiled=True)  44.6 us
    all_gather x1, waiting for transfers between devices, shards(): lax.all_gather(jnp.concatenate([block_in, original], axis=0), axis_id, ax...  40.5 us
    reduce_scatter x1, waiting for transfers between devices, shards(): lax.psum_scatter(grad_values.astype(jnp.bfloat16), 'ctx', scatter_dimensi...  40.3 us
  transfers between devices with their start and end apart: 13, of which 11 were waited for; matrix products, arithmetic and copies ran while one was open for 19% of the time, Pallas kernels for 0%

profile of v1, /device:TPU:0, one launch (start us, length us, event | category | flops | bytes accessed | tf_op | source)
XLA Modules:
  0.0 1118.6 jit_solution(4512615820760395736)
XLA Ops:
  14.7 42.5 %all-reduce.17 = (bf16[1536]{0:T(1024)(128)(2,1)S(1)}, bf16[768]{0:T(1024)(128)(2,1)S(1)}, bf16[768]{0:T(1024)(128)(2,1)S(1)}, bf16[768]{0:T(1024)(128)(2,1)S(1)...) all-reduce(bf16[1536]{0:T(1024)(128)(2,1)S(1)} %dynamic-update-slic, ...), channel_id=1, replica_groups=mesh['dp'=8,'ctx'=4] {'dp','ctx'}, use_global_device_ids=true, to_apply=%add | all-reduce | flops 9216 | bytes 36864
  57.3 16.5 %all-gather.10.cloned.1.call-done = bf16[768,2304]{1,0:T(8,128)(2,1)} async-done(((bf16[24,2304]{1,0:T(8,128)(2,1)}), bf16[768,2304]{1,0:T(8,128)(2,1)}) %all-gather.10.cloned.1.call-update) | async-done | bytes 3538960 | tf_op jit(solution)/shard_map/all_gather | solution.py:52
  87.6 40.5 %all-gather.12.cloned.1.call-done = bf16[2,2048,768]{2,1,0:T(8,128)(2,1)} async-done(((bf16[2,512,768]{2,1,0:T(8,128)(2,1)}), bf16[2,2048,768]{2,1,0:T(8,128)(2,1)}) %all-gather.12.cloned.1.call-update) | async-done | bytes 6291472 | tf_op jit(solution)/shard_map/all_gather | solution.py:122
  134.1 103.9 %while.30 = (s32[]{:T(128)}, f32[1,512,12,64]{1,3,2,0:T(8,128)}, f32[1,512,12]{1,2,0:T(8,128)S(1)}, f32[1,512,12]{1,2,0:T(8,128)S(1)}, s32[1,512]{1,0:T(1,128)S(...) while((s32[]{:T(128)}, f32[1,512,12,64]{1,3,2,0:T(8,128)}, ...), condition=%wide.region_3.4_spmd.clone, body=%wide.region_0.3_spmd.clone.sunk | while | flops 832213504 | bytes 50998480 | solution.py:146
  150.9 8.6 bitcast_add_fusion.6
  176.6 9.1 bitcast_add_fusion.6
  202.5 9.0 bitcast_add_fusion.6
  228.3 9.7 bitcast_add_fusion.6
  250.4 20.0 %multiply_convert_fusion = (bf16[512,3072]{1,0:T(8,128)(2,1)}, f32[512,3072]{1,0:T(8,128)}, f32[512,3072]{1,0:T(8,128)}) fusion(f32[3072]{0:T(1024)S(1)} %convert_element_type.115, bf16[768,3072]{1,0:T(8,128)(2,1)} %all-gather.16.cloned.1.call-done, f32[512,768]{1,0:T(8,128)S(1)} %get-tuple-element.445, f32[768]{0:T(1024)S(1)} %convert_element_type.113, ...), kind=kOutput, calls=%fused_computation.55 | convolution fusion | flops 2521694208 | bytes 22042624 | tf_op jit(solution)/shard_map/dot_general | solution.py:162
  270.4 44.6 %all-gather.18.cloned.1.call-done = bf16[3072,768]{1,0:T(8,128)(2,1)} async-done(((bf16[96,768]{1,0:T(8,128)(2,1)}), bf16[3072,768]{1,0:T(8,128)(2,1)}) %all-gather.18.cloned.1.call-update) | async-done | bytes 4718608 | tf_op jit(solution)/shard_map/all_gather | solution.py:60
  325.6 8.8 convert_reduce_fusion
  346.3 27.1 %all-gather.22.cloned.1.call-done = bf16[2048,768]{1,0:T(8,128)(2,1)} async-done(((bf16[512,768]{1,0:T(8,128)(2,1)}), bf16[2048,768]{1,0:T(8,128)(2,1)}) %all-gather.22.cloned.1.call-update) | async-done | bytes 3145744 | tf_op jit(solution)/shard_map/all_gather | solution.py:220
  377.5 142.6 %while.31 = (s32[]{:T(128)}, f32[1,512,12,64]{1,3,2,0:T(8,128)}, bf16[1,2048,768]{1,2,0:T(8,128)(2,1)}, bf16[1,2048,768]{1,2,0:T(8,128)(2,1)}, s32[4]{0:T(128)S(...) while((s32[]{:T(128)}, f32[1,512,12,64]{1,3,2,0:T(8,128)}, ...), condition=%wide.region_14.15_spmd.clone, body=%wide.region_13.14_spmd.clone.sunk | while | flops 2046034432 | bytes 114953560 | solution.py:251
  398.3 7.8 fusion.132
  469.5 7.8 fusion.132
  532.2 8.2 fusion.67
  542.0 16.0 %reduce-scatter.9.cloned.1.call-done = bf16[1,512,768]{1,2,0:T(8,128)(2,1)} async-done(((bf16[1,2048,768]{1,2,0:T(8,128)(2,1)}), bf16[1,512,768]{1,2,0:T(8,128)(2,1)}) %reduce-scatter.9.cloned.1.call-update) | async-done | bytes 786448 | tf_op jit(solution)/shard_map/reduce_scatter | solution.py:256
  558.0 40.3 %reduce-scatter.11.cloned.1.call-done = bf16[1,512,768]{1,2,0:T(8,128)(2,1)} async-done(((bf16[1,2048,768]{1,2,0:T(8,128)(2,1)}), bf16[1,512,768]{1,2,0:T(8,128)(2,1)}) %reduce-scatter.11.cloned.1.call-update) | async-done | bytes 786448 | tf_op jit(solution)/shard_map/reduce_scatter | solution.py:259
  604.5 8.0 copy.68
  615.7 40.2 %all-reduce.16 = (f32[1536]{0:T(1024)S(1)}, f32[768]{0:T(1024)S(1)}, f32[768]{0:T(1024)S(1)}, f32[768]{0:T(1024)S(1)}, f32[3072]{0:T(1024)S(1)}, /*index=5*/f32[...) all-reduce(f32[1536]{0:T(1024)S(1)} %pad_maximum_fusion.3, ...), channel_id=7, replica_groups=mesh['dp'=8,'ctx'=4] {'dp','ctx'}, use_global_device_ids=true, to_apply=%region_19.20.clone | all-reduce | flops 9216 | bytes 73728
  666.4 37.5 %reduce-scatter.13.cloned.1.call-done = f32[24,768]{1,0:T(8,128)} async-done(((f32[768,768]{1,0:T(8,128)}), f32[24,768]{1,0:T(8,128)}) %reduce-scatter.13.cloned.1.call-update) | async-done | bytes 73744 | tf_op jit(solution)/shard_map/reduce_scatter | solution.py:280
  703.9 141.7 %reduce-scatter.15.cloned.1.call-done = f32[24,3072]{1,0:T(8,128)} async-done(((f32[768,3072]{1,0:T(8,128)}), f32[24,3072]{1,0:T(8,128)}) %reduce-scatter.15.cloned.1.call-update) | async-done | bytes 294928 | tf_op jit(solution)/shard_map/reduce_scatter | solution.py:284
  845.6 141.5 %reduce-scatter.17.cloned.1.call-done = f32[96,768]{1,0:T(8,128)} async-done(((f32[3072,768]{1,0:T(8,128)}), f32[96,768]{1,0:T(8,128)}) %reduce-scatter.17.cloned.1.call-update) | async-done | bytes 294928 | tf_op jit(solution)/shard_map/reduce_scatter | solution.py:286
  987.1 124.8 %reduce-scatter.19.cloned.1.call-done = f32[24,2304]{1,0:T(8,128)} async-done(((f32[768,2304]{1,0:T(8,128)}), f32[24,2304]{1,0:T(8,128)}) %reduce-scatter.19.cloned.1.call-update) | async-done | bytes 221200
  (312 shorter events, 287.7 us)
Async XLA Ops:
  7.2 66.6 %all-gather.10.cloned.1.call-start = ((), (), s32[]{:S(2)}) async-start(), calls=%async_computation.6 | async-start | bytes 3649536 | tf_op jit(solution)/shard_map/all_gather | solution.py:52
  7.9 120.3 %all-gather.12.cloned.1.call-start = ((), (), s32[]{:S(2)}) async-start(), calls=%async_computation.7 | async-start | bytes 7864320 | tf_op jit(solution)/shard_map/all_gather | solution.py:122
  82.9 156.8 %all-gather.14.cloned.1.call-start = ((), (), s32[]{:S(2)}) async-start(), calls=%async_computation.8 | async-start | bytes 1216512 | tf_op jit(solution)/shard_map/all_gather | solution.py:54
  83.6 166.8 %all-gather.16.cloned.1.call-start = ((), (), s32[]{:S(2)}) async-start(), calls=%async_computation.9 | async-start | bytes 4866048 | tf_op jit(solution)/shard_map/all_gather | solution.py:58
  84.2 230.8 %all-gather.18.cloned.1.call-start = ((), (), s32[]{:S(2)}) async-start(), calls=%async_computation.10 | async-start | bytes 4866048 | tf_op jit(solution)/shard_map/all_gather | solution.py:60
  84.8 261.5 %all-gather.20.cloned.1.call-start = ((), (), s32[]{:S(2)}) async-start(), calls=%async_computation.16 | async-start | bytes 3932160 | tf_op jit(solution)/shard_map/all_gather | solution.py:219
  85.3 288.0 %all-gather.22.cloned.1.call-start = ((), (), s32[]{:S(2)}) async-start(), calls=%async_computation.17 | async-start | bytes 3932160 | tf_op jit(solution)/shard_map/all_gather | solution.py:220
  85.5 252.6 %copy-start.23 = (f32[768]{0:T(1024)}, f32[768]{0:T(1024)S(1)}, u32[]{:S(2)}) copy-start(f32[768]{0:T(1024)S(1)} %convert_element_type.112) | copy-start | bytes 9220
  85.5 229.5 %copy-start.30 = (f32[768]{0:T(1024)}, f32[768]{0:T(1024)S(1)}, u32[]{:S(2)}) copy-start(f32[768]{0:T(1024)S(1)} %convert_element_type.113) | copy-start | bytes 9220
  87.4 470.6 %reduce-scatter.9.cloned.1.call-start = ((), (), s32[]{:S(2)}) async-start(), calls=%async_computation.11 | async-start | bytes 3932160 | tf_op jit(solution)/shard_map/reduce_scatter | solution.py:256
  242.4 95.7 %copy-start.7 = (f32[512,768]{1,0:T(8,128)}, f32[512,768]{1,0:T(8,128)S(1)}, u32[]{:S(2)}) copy-start(f32[512,768]{1,0:T(8,128)S(1)} %get-tuple-element.445) | copy-start | bytes 4718596
  242.4 95.7 %copy-start.18 = (f32[512]{0:T(512)}, f32[512]{0:T(512)S(1)}, u32[]{:S(2)}) copy-start(f32[512]{0:T(512)S(1)} %broadcast_multiply_fusion.1) | copy-start | bytes 6148
  242.7 95.4 %copy-start.26 = (f32[512]{0:T(512)}, f32[512]{0:T(512)S(1)}, u32[]{:S(2)}) copy-start(f32[512]{0:T(512)S(1)} %fusion.50) | copy-start | bytes 6148
  324.4 10.0 slice-start
  325.2 9.2 copy-start.15
  325.6 8.8 slice-start.1
  520.1 78.2 %reduce-scatter.11.cloned.1.call-start = ((), (), s32[]{:S(2)}) async-start(), calls=%async_computation.12 | async-start | bytes 3932160 | tf_op jit(solution)/shard_map/reduce_scatter | solution.py:259
  520.9 182.9 %reduce-scatter.13.cloned.1.call-start = ((), (), s32[]{:S(2)}) async-start(), calls=%async_computation.13 | async-start | bytes 2433024 | tf_op jit(solution)/shard_map/reduce_scatter | solution.py:280
  523.7 321.9 %reduce-scatter.15.cloned.1.call-start = ((), (), s32[]{:S(2)}) async-start(), calls=%async_computation.14 | async-start | bytes 9732096 | tf_op jit(solution)/shard_map/reduce_scatter | solution.py:284
  531.1 455.9 %reduce-scatter.17.cloned.1.call-start = ((), (), s32[]{:S(2)}) async-start(), calls=%async_computation.15 | async-start | bytes 9732096 | tf_op jit(solution)/shard_map/reduce_scatter | solution.py:286
  540.4 57.9 %copy-start.36 = (bf16[1,512,768]{2,1,0:T(8,128)(2,1)S(1)}, bf16[1,512,768]{2,1,0:T(8,128)(2,1)}, u32[]{:S(2)}) copy-start(bf16[1,512,768]{2,1,0:T(8,128)(2,1)} %param.19) | copy-start | bytes 2359300
  540.5 571.4 %reduce-scatter.19.cloned.1.call-start = ((), (), s32[]{:S(2)}) async-start(), calls=%async_computation.18 | async-start | bytes 7299072
  612.6 47.9 %copy-start.10 = (f32[512,768]{1,0:T(8,128)S(1)}, f32[512,768]{1,0:T(8,128)}, u32[]{:S(2)}) copy-start(f32[512,768]{1,0:T(8,128)} %copy-done.9) | copy-start | bytes 4718596
  612.7 47.9 %copy-start.29 = (f32[512]{0:T(512)S(1)}, f32[512]{0:T(512)}, u32[]{:S(2)}) copy-start(f32[512]{0:T(512)} %copy-done.28) | copy-start | bytes 6148
  (38 other events, 101.2 us)
Sparse Core Ops, SparseCore 0:
  10.9 62.7 all-gather.9
  83.0 45.1 all-gather.11
  131.1 53.9 all-gather.13
  187.9 62.4 all-gather.15
  253.1 61.8 all-gather.17
  316.4 26.8 all-gather.19
  344.8 28.4 all-gather.21
  520.2 37.7 reduce-scatter.8
  560.5 37.7 reduce-scatter.10
  604.0 99.8 reduce-scatter.12
  710.3 135.2 reduce-scatter.14
  851.9 135.0 reduce-scatter.16
  993.3 118.5 reduce-scatter.18
